TPU v7x, 512 devices: a whole 4x4x16 slice. The times are simulated.
512 devices in a mesh: test: 8 (over z_lo, core), bx: 4 (over y), by: 16 (over z_hi, x).
Axes of the slice: x: 4, y: 4, z: 16 (z_hi: 4, z_lo: 4; z = z_hi * 4 + z_lo), core: 2. Of those that a mesh axis runs over, the one named last changes fastest.
Arguments:
- log_conductivity: float32 [32, 128, 256], P('bx', 'by'), may hold values from -3 to 3
- storage: float32 [32, 128, 256], P('bx', 'by'), may hold values from 0.5 to 2
- recharge: float32 [32, 128, 256], P('bx', 'by'), may hold values from -6 to 6
- pump_rate: float32 [32], P('test'), may hold values from 4 to 16
- pump_well: int32 [32], P('test'), may hold values from 0 to 2047
- observed: float32 [32, 2048], P('test'), may hold values from -9 to 9
- owner: int32 [2048], replicated, may hold values from 0 to 63, as said below
- screen_column: int32 [2048], replicated, may hold values from 0 to 63
- screen_top: int32 [2048], replicated, may hold values from 0 to 248
Outputs:
- gradient: float32 [32, 128, 256], P('bx', 'by', 'test')
Inputs may be any that keep to these rules, and one draw needn't show every extreme that they name: `owner`: each brick owns exactly 32 wells.
All inputs are finite; a program needn't handle non-finite values.
Results may differ from a plain program's by a relative error of at most 0.0001.
Values sent between devices are 32-bit elements; how exact they have to be, the bound alone decides.
A program may use at most 64 MiB of HBM per device.

v0:
```python
import jax
import jax.numpy as jnp
from jax import lax
from jax.sharding import PartitionSpec as P

SWEEPS = 3
SCREEN = 8
epsilon = 1e-06


def with_halo(block, sides, width):
    for axis, dim in sides:
        count = lax.axis_size(axis)
        forward = [(i, i + 1) for i in range(count - 1)]
        backward = [(target, source) for source, target in forward]
        low = lax.ppermute(
            lax.slice_in_dim(block, block.shape[dim] - width, None, axis=dim), axis, forward
        )
        high = lax.ppermute(lax.slice_in_dim(block, 0, width, axis=dim), axis, backward)
        block = jnp.concatenate([low, block, high], axis=dim)
    return block


def pad_depth(values):
    return jnp.pad(values, [(0, 0)] * (values.ndim - 1) + [(1, 1)])


def neighbours(padded, centre):
    z_padded = pad_depth(centre)
    return [
        padded[..., 2:, 1:-1, :],
        padded[..., :-2, 1:-1, :],
        padded[..., 1:-1, 2:, :],
        padded[..., 1:-1, :-2, :],
        z_padded[..., 2:],
        z_padded[..., :-2],
    ]


def weighted(conductance, others):
    accumulated = conductance[0] * others[0]
    for position in range(1, 6):
        accumulated = accumulated + conductance[position] * others[position]
    return accumulated


def sensitivity(conductance, heads_field, heads_padded, adjoint_field, adjoint_padded):
    near_heads = neighbours(heads_padded, heads_field)
    near_adjoint = neighbours(adjoint_padded, adjoint_field)
    accumulated = jnp.zeros_like(heads_field)
    for position in range(6):
        accumulated = accumulated + conductance[position] * (heads_field - near_heads[position]) * (
            adjoint_field - near_adjoint[position]
        )
    return -0.5 * accumulated


def relax_field(source, conductance, diagonal):
    iterate = source / diagonal
    for sweep_index in range(SWEEPS - 1):
        padded = with_halo(iterate, (("bx", 1), ("by", 2)), 1)
        iterate = (source + weighted(conductance, neighbours(padded, iterate))) / diagonal
    return iterate


def per_sweep_terms(
    log_conductivity,
    storage,
    recharge,
    pump_rate,
    pump_well,
    observed,
    owner,
    screen_column,
    screen_top,
):
    size_x, size_y, size_z = log_conductivity.shape
    tests_here = pump_rate.shape[0]
    cell_count = size_x * size_y * size_z
    padded_log = with_halo(log_conductivity, (("bx", 0), ("by", 1)), 1)
    conductance = [
        jnp.exp(0.5 * (log_conductivity + other))
        for other in neighbours(padded_log, log_conductivity)
    ]
    diagonal = storage + weighted(conductance, [1.0] * 6)
    brick_index = lax.axis_index("bx") * lax.axis_size("by") + lax.axis_index("by")
    offsets = jnp.arange(SCREEN, dtype=jnp.int32)
    screen_cells = (screen_column * size_z + screen_top)[:, None] + offsets[None, :]
    owned_here = owner == brick_index
    pump_cells = screen_cells[pump_well]
    pump_value = jnp.where(owner[pump_well] == brick_index, -pump_rate, 0.0)
    test_rows = jnp.arange(tests_here, dtype=jnp.int32)[:, None]
    flat_source = jnp.broadcast_to(recharge.reshape(1, cell_count), (tests_here, cell_count))
    flat_source = flat_source.at[test_rows, pump_cells].add(
        jnp.broadcast_to(pump_value[:, None], pump_cells.shape)
    )
    source = flat_source.reshape(tests_here, size_x, size_y, size_z)
    heads_field = relax_field(source, conductance, diagonal)
    well_heads = jnp.mean(heads_field.reshape(tests_here, cell_count)[:, screen_cells], axis=2)
    residual = jnp.where(owned_here[None, :], well_heads - observed, 0.0)
    well_count = residual.shape[1]
    misfit = lax.psum(jnp.sum(residual * residual, axis=1), ("bx", "by")) / well_count + epsilon
    weights = residual / misfit[:, None]
    values = jnp.broadcast_to(weights[:, :, None], (tests_here, well_count, SCREEN)).reshape(
        tests_here, -1
    )
    adjoint_source = (
        jnp.zeros((tests_here, cell_count), jnp.float32).at[:, screen_cells.reshape(-1)].add(values)
    )
    adjoint_field = relax_field(
        adjoint_source.reshape(tests_here, size_x, size_y, size_z), conductance, diagonal
    )
    stacked = with_halo(
        jnp.concatenate([heads_field, adjoint_field], axis=0), (("bx", 1), ("by", 2)), 1
    )
    test_terms = sensitivity(
        conductance, heads_field, stacked[:tests_here], adjoint_field, stacked[tests_here:]
    )
    return (test_terms, misfit)


def local(
    log_conductivity,
    storage,
    recharge,
    pump_rate,
    pump_well,
    observed,
    owner,
    screen_column,
    screen_top,
):
    size_z = log_conductivity.shape[2]
    tests_here = pump_rate.shape[0]
    test_terms, misfit = per_sweep_terms(
        log_conductivity,
        storage,
        recharge,
        pump_rate,
        pump_well,
        observed,
        owner,
        screen_column,
        screen_top,
    )
    local_sum = jnp.sum(test_terms, axis=0)
    all_tests = tests_here * lax.axis_size("test")
    grand_total = lax.psum(local_sum, "test")
    slab_depth = size_z // lax.axis_size("test")
    gradient = lax.dynamic_slice_in_dim(
        grand_total, lax.axis_index("test") * slab_depth, slab_depth, 2
    )
    return gradient / all_tests


def solution(mesh):
    placed = (
        P("bx", "by", None),
        P("bx", "by", None),
        P("bx", "by", None),
        P("test"),
        P("test"),
        P("test", None),
        P(),
        P(),
        P(),
    )
    return jax.shard_map(
        local, mesh=mesh, in_specs=placed, out_specs=P("bx", "by", "test"), check_vma=False
    )
```

profile of v0, /device:TPU:2, one launch (start us, length us, event | category | flops | bytes accessed | tf_op | source)
XLA Modules:
  0.0 626.8 jit_solution(6473687219000279522)
XLA Ops:
  7.3 3.5 collective-permute-start.1
  16.6 5.6 collective-permute-start.2
  22.2 1.9 collective-permute-start.3
  26.0 2.1 scatter_fusion
  30.8 5.2 collective-permute-start.5
  37.6 3.9 collective-permute-start.6
  41.5 1.9 collective-permute-start.7
  44.3 3.1 collective-permute-done.7
  50.4 4.9 collective-permute-start.9
  56.9 1.9 collective-permute-start.10
  58.8 4.6 collective-permute-start.11
  65.4 4.7 copy.20
  70.1 58.2 %gather_fusion.2 = f32[16384,4]{1,0:T(8,128)} fusion(f32[4,16384]{0,1:T(8,128)} %bitcast.34, s32[16384]{0:T(1024)S(1)} %broadcast_clamp_fusion), kind=kCustom, calls=%fused_computation.2 | custom fusion | bytes 589824 | tf_op jit(solution)/shard_map/gather | solution.py:99
  128.3 13.0 %bitcast_reduce_fusion = f32[2048,4]{1,0:T(8,128)S(1)} fusion(f32[16384,4]{1,0:T(8,128)} %gather_fusion.2), kind=kLoop, calls=%fused_computation.7 | loop fusion | flops 57344 | bytes 294912 | tf_op jit(solution)/shard_map/reduce_sum | solution.py:99
  142.5 236.4 %psum.14 = f32[4]{0:T(128)S(1)} all-reduce(f32[4]{0:T(128)S(1)} %multiply_reduce_fusion), channel_id=1, replica_groups=mesh['test'=8,'bx'=4,'by'=16] {'bx','by'}, use_global_device_ids=true, to_apply=%region_3.4 | all-reduce | flops 4 | bytes 32 | tf_op jit(solution)/shard_map/psum | solution.py:102
  379.4 91.6 %scatter_custom_fusion.1 = f32[4,16384]{0,1:T(8,128)} fusion(s32[16384]{0:T(1024)} %bitcast.41, f32[4,2048]{0,1:T(8,128)S(1)} %broadcast_divide_fusion, f32[]{:T(128)} %constant.27.clone.1), kind=kCustom, calls=%fused_computation.5 | custom fusion | flops 65536 | bytes 295424 | tf_op jit(solution)/shard_map/scatter-add | solution.py:108
  471.0 5.2 copy.24
  477.6 4.5 collective-permute-start.13
  482.1 1.6 collective-permute-done.13
  483.8 4.0 collective-permute-start.14
  487.8 1.9 collective-permute-start.15
  489.7 4.0 collective-permute-done.15
  495.2 4.9 collective-permute-start.17
  501.7 1.9 collective-permute-start.18
  503.7 3.9 collective-permute-start.19
  507.6 1.9 collective-permute-done.19
  511.1 4.9 collective-permute-start.21
  516.3 1.6 collective-permute-done.21
  518.0 1.9 collective-permute-start.22
  519.9 3.9 collective-permute-start.23
  524.3 1.9 collective-permute-done.23
  527.4 91.2 %all-reduce.9.cloned.1.call-done = f32[8,8,256]{2,1,0:T(8,128)} async-done(((f32[8,8,256]{2,1,0:T(8,128)}), f32[8,8,256]{2,1,0:T(8,128)}) %all-reduce.9.cloned.1.call-update) | async-done | bytes 65552 | tf_op jit(solution)/shard_map/psum | solution.py:148
  (99 shorter events, 31.1 us)
Async XLA Ops:
  6.5 56.9 %copy-start = (s32[2048]{0:T(1024)S(1)}, s32[2048]{0:T(1024)}, u32[]{:S(2)}) copy-start(s32[2048]{0:T(1024)} %param.15) | copy-start | bytes 24580
  6.5 612.0 %all-reduce.9.cloned.1.call-start = ((), (), s32[]{:S(2)}) async-start(), calls=%async_computation | async-start | bytes 131072 | tf_op jit(solution)/shard_map/psum | solution.py:148
  7.3 8.4 %collective-permute-start.1 = (f32[1,8,256]{2,1,0:T(8,128)S(1)}, f32[1,8,256]{2,1,0:T(8,128)S(1)}, u32[]{:S(2)}, u32[]{:S(2)}) collective-permute-start(f32[1,8,256]{2,1,0:T(8,128)S(1)} %get-tuple-element.35), channel_id=1, source_target_pairs={{0,16},{16,32},{32,48},{1,17},{17,33},{33,49},{2,18},{18,34},{34,5... | collective-permute-start | bytes 24584 | tf_op jit(solution)/shard_map/ppermute | solution.py:16
  10.7 5.8 collective-permute-start
  16.6 11.5 %collective-permute-start.2 = (f32[10,1,256]{2,1,0:T(1,128)S(1)}, f32[10,1,256]{2,1,0:T(1,128)S(1)}, u32[]{:S(2)}, u32[]{:S(2)}) collective-permute-start(f32[10,1,256]{2,1,0:T(1,128)S(1)} %get-tuple-element.33), channel_id=1, source_target_pairs={{1,0},{2,1},{3,2},{4,3},{5,4},{6,5},{7,6},{8,7},{9,8},{10,9},{11,1... | collective-permute-start | bytes 30728 | tf_op jit(solution)/shard_map/ppermute | solution.py:19
  22.2 5.9 collective-permute-start.3
  29.3 40.8 %copy-start.1 = (f32[8,8,256]{2,1,0:T(8,128)}, f32[8,8,256]{2,1,0:T(8,128)S(1)}, u32[]{:S(2)}) copy-start(f32[8,8,256]{2,1,0:T(8,128)S(1)} %get-tuple-element.7) | copy-start | bytes 196612
  29.5 6.5 %collective-permute-start.4 = (f32[4,1,8,256]{3,2,1,0:T(8,128)S(1)}, f32[4,1,8,256]{3,2,1,0:T(8,128)S(1)}, u32[]{:S(2)}, u32[]{:S(2)}) collective-permute-start(f32[4,1,8,256]{3,2,1,0:T(8,128)S(1)} %get-tuple-element.31), channel_id=1, source_target_pairs={{16,0},{32,16},{48,32},{17,1},{33,17},{49,33},{18,2},{34,18},{50,3... | collective-permute-start | bytes 98312 | tf_op jit(solution)/shard_map/ppermute | solution.py:19
  30.8 6.8 %collective-permute-start.5 = (f32[4,1,8,256]{3,2,1,0:T(8,128)S(1)}, f32[4,1,8,256]{3,2,1,0:T(8,128)S(1)}, u32[]{:S(2)}, u32[]{:S(2)}) collective-permute-start(f32[4,1,8,256]{3,2,1,0:T(8,128)S(1)} %get-tuple-element.30), channel_id=1, source_target_pairs={{0,16},{16,32},{32,48},{1,17},{17,33},{33,49},{2,18},{18,34},{34,5... | collective-permute-start | bytes 98312 | tf_op jit(solution)/shard_map/ppermute | solution.py:16
  37.6 6.7 %collective-permute-start.6 = (f32[4,10,1,256]{3,2,1,0:T(1,128)S(1)}, f32[4,10,1,256]{3,2,1,0:T(1,128)S(1)}, u32[]{:S(2)}, u32[]{:S(2)}) collective-permute-start(f32[4,10,1,256]{3,2,1,0:T(1,128)S(1)} %get-tuple-element.22), channel_id=1, source_target_pairs={{1,0},{2,1},{3,2},{4,3},{5,4},{6,5},{7,6},{8,7},{9,8},{10,9},{11,1... | collective-permute-start | bytes 122888 | tf_op jit(solution)/shard_map/ppermute | solution.py:19
  41.5 5.9 collective-permute-start.7
  49.1 6.2 collective-permute-start.8
  50.4 6.4 %collective-permute-start.9 = (f32[4,1,8,256]{3,2,1,0:T(8,128)S(1)}, f32[4,1,8,256]{3,2,1,0:T(8,128)S(1)}, u32[]{:S(2)}, u32[]{:S(2)}) collective-permute-start(f32[4,1,8,256]{3,2,1,0:T(8,128)S(1)} %get-tuple-element.28), channel_id=1, source_target_pairs={{0,16},{16,32},{32,48},{1,17},{17,33},{33,49},{2,18},{18,34},{34,5... | collective-permute-start | bytes 98312 | tf_op jit(solution)/shard_map/ppermute | solution.py:16
  56.9 8.2 %collective-permute-start.10 = (f32[4,10,1,256]{3,2,1,0:T(1,128)S(1)}, f32[4,10,1,256]{3,2,1,0:T(1,128)S(1)}, u32[]{:S(2)}, u32[]{:S(2)}) collective-permute-start(f32[4,10,1,256]{3,2,1,0:T(1,128)S(1)} %get-tuple-element.20), channel_id=1, source_target_pairs={{1,0},{2,1},{3,2},{4,3},{5,4},{6,5},{7,6},{8,7},{9,8},{10,9},{11,1... | collective-permute-start | bytes 122888 | tf_op jit(solution)/shard_map/ppermute | solution.py:19
  58.8 6.3 %collective-permute-start.11 = (f32[4,10,1,256]{3,2,1,0:T(1,128)S(1)}, f32[4,10,1,256]{3,2,1,0:T(1,128)S(1)}, u32[]{:S(2)}, u32[]{:S(2)}) collective-permute-start(f32[4,10,1,256]{3,2,1,0:T(1,128)S(1)} %get-tuple-element.21), channel_id=1, source_target_pairs={{0,1},{1,2},{2,3},{3,4},{4,5},{5,6},{6,7},{7,8},{8,9},{9,10},{10,1... | collective-permute-start | bytes 122888 | tf_op jit(solution)/shard_map/ppermute | solution.py:16
  379.4 114.3 %copy-start.2 = (f32[8,8,256]{2,1,0:T(8,128)S(1)}, f32[8,8,256]{2,1,0:T(8,128)}, u32[]{:S(2)}) copy-start(f32[8,8,256]{2,1,0:T(8,128)} %copy-done.1) | copy-start | bytes 196612
  379.4 114.3 %copy-start.4 = (f32[8,8,256]{2,1,0:T(8,128)S(1)}, f32[8,8,256]{2,1,0:T(8,128)}, u32[]{:S(2)}) copy-start(f32[8,8,256]{2,1,0:T(8,128)} %copy-done.3) | copy-start | bytes 196612
  379.4 114.3 %copy-start.6 = (f32[8,8,256]{2,1,0:T(8,128)S(1)}, f32[8,8,256]{2,1,0:T(8,128)}, u32[]{:S(2)}) copy-start(f32[8,8,256]{2,1,0:T(8,128)} %copy-done.5) | copy-start | bytes 196612
  379.4 114.3 %copy-start.8 = (f32[8,8,256]{2,1,0:T(8,128)S(1)}, f32[8,8,256]{2,1,0:T(8,128)}, u32[]{:S(2)}) copy-start(f32[8,8,256]{2,1,0:T(8,128)} %copy-done.7) | copy-start | bytes 196612
  379.4 114.3 %copy-start.10 = (f32[8,8,256]{2,1,0:T(8,128)S(1)}, f32[8,8,256]{2,1,0:T(8,128)}, u32[]{:S(2)}) copy-start(f32[8,8,256]{2,1,0:T(8,128)} %copy-done.9) | copy-start | bytes 196612
  476.3 5.9 collective-permute-start.12
  477.6 6.1 collective-permute-start.13
  483.8 5.9 collective-permute-start.14
  487.8 5.9 collective-permute-start.15
  493.9 6.2 collective-permute-start.16
  495.2 6.4 %collective-permute-start.17 = (f32[4,1,8,256]{3,2,1,0:T(8,128)S(1)}, f32[4,1,8,256]{3,2,1,0:T(8,128)S(1)}, u32[]{:S(2)}, u32[]{:S(2)}) collective-permute-start(f32[4,1,8,256]{3,2,1,0:T(8,128)S(1)} %get-tuple-element.24), channel_id=1, source_target_pairs={{0,16},{16,32},{32,48},{1,17},{17,33},{33,49},{2,18},{18,34},{34,5... | collective-permute-start | bytes 98312 | tf_op jit(solution)/shard_map/ppermute | solution.py:16
  501.7 5.9 collective-permute-start.18
  503.7 5.9 collective-permute-start.19
  509.8 6.5 %collective-permute-start.20 = (f32[8,1,8,256]{3,2,1,0:T(8,128)S(1)}, f32[8,1,8,256]{3,2,1,0:T(8,128)S(1)}, u32[]{:S(2)}, u32[]{:S(2)}) collective-permute-start(f32[8,1,8,256]{3,2,1,0:T(8,128)S(1)} %get-tuple-element.15), channel_id=1, source_target_pairs={{16,0},{32,16},{48,32},{17,1},{33,17},{49,33},{18,2},{34,18},{50,3... | collective-permute-start | bytes 196616 | tf_op jit(solution)/shard_map/ppermute | solution.py:19
  511.1 6.7 %collective-permute-start.21 = (f32[8,1,8,256]{3,2,1,0:T(8,128)S(1)}, f32[8,1,8,256]{3,2,1,0:T(8,128)S(1)}, u32[]{:S(2)}, u32[]{:S(2)}) collective-permute-start(f32[8,1,8,256]{3,2,1,0:T(8,128)S(1)} %get-tuple-element.14), channel_id=1, source_target_pairs={{0,16},{16,32},{32,48},{1,17},{17,33},{33,49},{2,18},{18,34},{34,5... | collective-permute-start | bytes 196616 | tf_op jit(solution)/shard_map/ppermute | solution.py:16
  518.0 6.3 %collective-permute-start.22 = (f32[8,10,1,256]{3,2,1,0:T(1,128)S(1)}, f32[8,10,1,256]{3,2,1,0:T(1,128)S(1)}, u32[]{:S(2)}, u32[]{:S(2)}) collective-permute-start(f32[8,10,1,256]{3,2,1,0:T(1,128)S(1)} %get-tuple-element.12), channel_id=1, source_target_pairs={{1,0},{2,1},{3,2},{4,3},{5,4},{6,5},{7,6},{8,7},{9,8},{10,9},{11,1... | collective-permute-start | bytes 245768 | tf_op jit(solution)/shard_map/ppermute | solution.py:19
  519.9 6.3 %collective-permute-start.23 = (f32[8,10,1,256]{3,2,1,0:T(1,128)S(1)}, f32[8,10,1,256]{3,2,1,0:T(1,128)S(1)}, u32[]{:S(2)}, u32[]{:S(2)}) collective-permute-start(f32[8,10,1,256]{3,2,1,0:T(1,128)S(1)} %get-tuple-element.13), channel_id=1, source_target_pairs={{0,1},{1,2},{2,3},{3,4},{4,5},{5,6},{6,7},{7,8},{8,9},{9,10},{10,1... | collective-permute-start | bytes 245768 | tf_op jit(solution)/shard_map/ppermute | solution.py:16
  (6 other events, 166.8 us)
Sparse Core Ops, SparseCore 0:
  527.5 90.9 all-reduce.8
where the time goes:
time: 628 us; the launch traced here: 627 us
  blocking collectives  236 us (38%)
  other arithmetic  117 us (19%)
  waiting for transfers between devices  111 us (18%)
  local copies, waits for them, and re-layouts  75.6 us (12%)
  starting transfers between devices  73 us (12%)
  between operations  14 us (2%)
    psum x1, blocking collectives, per_sweep_terms(): lax.psum(jnp.sum(residual * residual, axis=1), ('bx', 'by')) / well_count  236 us
    scatter-add x1, other arithmetic, per_sweep_terms(): jnp.zeros((tests_here, cell_count), jnp.float32)  91.6 us
    psum x1, waiting for transfers between devices, local(): grand_total = lax.psum(local_sum, 'test')  91.2 us
    gather x1, local copies, waits for them, and re-layouts, per_sweep_terms(): heads_field.reshape(tests_here, cell_count)[:, screen_cells]  58.2 us
    ppermute x12, starting transfers between devices, with_halo(): lax.ppermute(lax.slice_in_dim(block, block.shape[dim] - width, None, axis...  45.9 us
    ppermute x12, starting transfers between devices, with_halo(): lax.ppermute(lax.slice_in_dim(block, 0, width, axis=dim), axis, backward)  27.1 us
    ppermute x12, waiting for transfers between devices, with_halo(): lax.ppermute(lax.slice_in_dim(block, block.shape[dim] - width, None, axis...  18.8 us
    reduce_sum x1, other arithmetic, per_sweep_terms(): jnp.mean(heads_field.reshape(tests_here, cell_count)[:, screen_cells], ax...  13 us
  transfers between devices with their start and end apart: 25, of which 12 were waited for; matrix products, arithmetic and copies ran while one was open for 2% of the time, Pallas kernels for 0%

commit v1 on v0

--- a/solution.py
+++ b/solution.py
@@ -6,6 +6,7 @@
 SWEEPS = 3
 SCREEN = 8
 epsilon = 1e-06
+follow_domain_in = lambda sheet: lax.psum(lax.psum(sheet, "bx"), "by")
 
 
 def with_halo(block, sides, width):
@@ -99,7 +100,7 @@
     well_heads = jnp.mean(heads_field.reshape(tests_here, cell_count)[:, screen_cells], axis=2)
     residual = jnp.where(owned_here[None, :], well_heads - observed, 0.0)
     well_count = residual.shape[1]
-    misfit = lax.psum(jnp.sum(residual * residual, axis=1), ("bx", "by")) / well_count + epsilon
+    misfit = follow_domain_in(jnp.sum(residual * residual, axis=1)) / well_count + epsilon
     weights = residual / misfit[:, None]
     values = jnp.broadcast_to(weights[:, :, None], (tests_here, well_count, SCREEN)).reshape(
         tests_here, -1

time: 628 us -> 483 us (0.77)
  blocking collectives: 236 us -> 78.2 us
  waiting for transfers between devices: 111 us -> 123 us
    psum x1 -> x2, blocking collectives: 236 us -> 78.2 us  [follow_domain_in = lambda sheet: lax.psum(lax.psum(sheet, 'bx'), 'by')]
    psum x1, waiting for transfers between devices: 91.2 us -> 103 us  [local(): grand_total = lax.psum(local_sum, 'test')]
  transfers between devices with their start and end apart: 25 -> 25, of which waited for: 12 -> 13; matrix products, arithmetic and copies ran while one was open for 2% -> 2% of each run, Pallas kernels for 0% -> 0%
where the time goes in v1:
time: 483 us; the launch traced here: 482 us
  waiting for transfers between devices  123 us (25%)
  other arithmetic  118 us (24%)
  blocking collectives  78.2 us (16%)
  local copies, waits for them, and re-layouts  74.9 us (16%)
  starting transfers between devices  72.9 us (15%)
  between operations  14 us (3%)
    psum x1, waiting for transfers between devices, local(): grand_total = lax.psum(local_sum, 'test')  103 us
    scatter-add x1, other arithmetic, per_sweep_terms(): jnp.zeros((tests_here, cell_count), jnp.float32)  91.6 us
    psum x2, blocking collectives, follow_domain_in = lambda sheet: lax.psum(lax.psum(sheet, 'bx'), 'by')  78.2 us
    gather x1, local copies, waits for them, and re-layouts, per_sweep_terms(): heads_field.reshape(tests_here, cell_count)[:, screen_cells]  58.1 us
    ppermute x12, starting transfers between devices, with_halo(): lax.ppermute(lax.slice_in_dim(block, block.shape[dim] - width, None, axis...  45.9 us
    ppermute x12, starting transfers between devices, with_halo(): lax.ppermute(lax.slice_in_dim(block, 0, width, axis=dim), axis, backward)  27 us
    ppermute x12, waiting for transfers between devices, with_halo(): lax.ppermute(lax.slice_in_dim(block, block.shape[dim] - width, None, axis...  19.9 us
    reduce_sum x1, other arithmetic, per_sweep_terms(): jnp.mean(heads_field.reshape(tests_here, cell_count)[:, screen_cells], ax...  13 us
  transfers between devices with their start and end apart: 25, of which 13 were waited for; matrix products, arithmetic and copies ran while one was open for 2% of the time, Pallas kernels for 0%

profile of v1, /device:TPU:2, one launch (start us, length us, event | category | flops | bytes accessed | tf_op | source)
XLA Modules:
  0.0 481.6 jit_solution(11520950937153014484)
XLA Ops:
  7.3 3.5 collective-permute-start.1
  16.6 5.6 %collective-permute-start.2 = (f32[10,1,256]{2,1,0:T(1,128)S(1)}, f32[10,1,256]{2,1,0:T(1,128)S(1)}, u32[]{:S(2)}, u32[]{:S(2)}) collective-permute-start(f32[10,1,256]{2,1,0:T(1,128)S(1)} %get-tuple-element.33), channel_id=1, source_target_pairs={{1,0},{2,1},{3,2},{4,3},{5,4},{6,5},{7,6},{8,7},{9,8},{10,9},{11,1... | collective-permute-start | bytes 30728 | tf_op jit(solution)/shard_map/ppermute | solution.py:20
  22.2 1.9 collective-permute-start.3
  26.0 2.1 scatter_fusion
  30.8 5.2 %collective-permute-start.5 = (f32[4,1,8,256]{3,2,1,0:T(8,128)S(1)}, f32[4,1,8,256]{3,2,1,0:T(8,128)S(1)}, u32[]{:S(2)}, u32[]{:S(2)}) collective-permute-start(f32[4,1,8,256]{3,2,1,0:T(8,128)S(1)} %get-tuple-element.30), channel_id=1, source_target_pairs={{0,16},{16,32},{32,48},{1,17},{17,33},{33,49},{2,18},{18,34},{34,5... | collective-permute-start | bytes 98312 | tf_op jit(solution)/shard_map/ppermute | solution.py:17
  37.6 3.9 collective-permute-start.6
  41.5 1.9 collective-permute-start.7
  44.3 3.1 collective-permute-done.7
  49.0 4.9 %collective-permute-start.9 = (f32[4,1,8,256]{3,2,1,0:T(8,128)S(1)}, f32[4,1,8,256]{3,2,1,0:T(8,128)S(1)}, u32[]{:S(2)}, u32[]{:S(2)}) collective-permute-start(f32[4,1,8,256]{3,2,1,0:T(8,128)S(1)} %get-tuple-element.28), channel_id=1, source_target_pairs={{0,16},{16,32},{32,48},{1,17},{17,33},{33,49},{2,18},{18,34},{34,5... | collective-permute-start | bytes 98312 | tf_op jit(solution)/shard_map/ppermute | solution.py:17
  55.5 1.9 collective-permute-start.10
  57.4 4.6 collective-permute-start.11
  64.9 4.7 copy.20
  69.7 58.1 %gather_fusion.2 = f32[16384,4]{1,0:T(8,128)} fusion(f32[4,16384]{0,1:T(8,128)} %bitcast.34, s32[16384]{0:T(1024)S(1)} %broadcast_clamp_fusion), kind=kCustom, calls=%fused_computation.2 | custom fusion | bytes 589824 | tf_op jit(solution)/shard_map/gather | solution.py:100
  127.8 13.0 %bitcast_reduce_fusion = f32[2048,4]{1,0:T(8,128)S(1)} fusion(f32[16384,4]{1,0:T(8,128)} %gather_fusion.2), kind=kLoop, calls=%fused_computation.7 | loop fusion | flops 57344 | bytes 294912 | tf_op jit(solution)/shard_map/reduce_sum | solution.py:100
  142.4 12.6 %psum.21 = f32[4]{0:T(128)S(1)} all-reduce(f32[4]{0:T(128)S(1)} %multiply_reduce_fusion), channel_id=1, replica_groups=mesh['test'=8,'bx'=4,'by'=16] {'bx'}, use_global_device_ids=true, to_apply=%region_3.4 | all-reduce | flops 4 | bytes 32 | tf_op jit(solution)/shard_map/psum | solution.py:9
  156.6 65.6 %psum.22 = f32[4]{0:T(128)S(1)} all-reduce(f32[4]{0:T(128)S(1)} %psum.21), channel_id=1, replica_groups=mesh['test'=8,'bx'=4,'by'=16] {'by'}, use_global_device_ids=true, to_apply=%region_4.5 | all-reduce | flops 4 | bytes 32 | tf_op jit(solution)/shard_map/psum | solution.py:9
  222.7 91.6 %scatter_custom_fusion.1 = f32[4,16384]{0,1:T(8,128)} fusion(s32[16384]{0:T(1024)} %bitcast.41, f32[4,2048]{0,1:T(8,128)S(1)} %broadcast_divide_fusion, f32[]{:T(128)} %constant.27.clone.1), kind=kCustom, calls=%fused_computation.5 | custom fusion | flops 65536 | bytes 295424 | tf_op jit(solution)/shard_map/scatter-add | solution.py:109
  314.2 5.2 %copy.24 = f32[4,8,8,256]{3,2,1,0:T(8,128)S(1)} copy(f32[4,8,8,256]{0,3,2,1:T(8,128)} %bitcast.38) | data formatting | bytes 524288 | tf_op jit(solution)/shard_map/reshape | solution.py:112
  320.8 4.5 collective-permute-start.13
  327.0 3.9 collective-permute-start.14
  330.9 1.9 collective-permute-start.15
  332.9 3.9 collective-permute-done.15
  338.4 4.9 %collective-permute-start.17 = (f32[4,1,8,256]{3,2,1,0:T(8,128)S(1)}, f32[4,1,8,256]{3,2,1,0:T(8,128)S(1)}, u32[]{:S(2)}, u32[]{:S(2)}) collective-permute-start(f32[4,1,8,256]{3,2,1,0:T(8,128)S(1)} %get-tuple-element.24), channel_id=1, source_target_pairs={{0,16},{16,32},{32,48},{1,17},{17,33},{33,49},{2,18},{18,34},{34,5... | collective-permute-start | bytes 98312 | tf_op jit(solution)/shard_map/ppermute | solution.py:17
  344.9 1.9 collective-permute-start.18
  346.9 3.9 collective-permute-start.19
  350.8 1.9 collective-permute-done.19
  354.3 4.9 %collective-permute-start.21 = (f32[8,1,8,256]{3,2,1,0:T(8,128)S(1)}, f32[8,1,8,256]{3,2,1,0:T(8,128)S(1)}, u32[]{:S(2)}, u32[]{:S(2)}) collective-permute-start(f32[8,1,8,256]{3,2,1,0:T(8,128)S(1)} %get-tuple-element.14), channel_id=1, source_target_pairs={{0,16},{16,32},{32,48},{1,17},{17,33},{33,49},{2,18},{18,34},{34,5... | collective-permute-start | bytes 196616 | tf_op jit(solution)/shard_map/ppermute | solution.py:17
  359.5 1.6 collective-permute-done.21
  361.2 1.9 collective-permute-start.22
  363.1 3.9 collective-permute-start.23
  367.5 1.9 collective-permute-done.23
  370.6 102.7 %all-reduce.9.cloned.1.call-done = f32[8,8,256]{2,1,0:T(8,128)} async-done(((f32[8,8,256]{2,1,0:T(8,128)}), f32[8,8,256]{2,1,0:T(8,128)}) %all-reduce.9.cloned.1.call-update) | async-done | bytes 65552 | tf_op jit(solution)/shard_map/psum | solution.py:149
  (98 shorter events, 34.2 us)
Async XLA Ops:
  6.5 55.5 %copy-start = (s32[2048]{0:T(1024)S(1)}, s32[2048]{0:T(1024)}, u32[]{:S(2)}) copy-start(s32[2048]{0:T(1024)} %param.15) | copy-start | bytes 24580
  6.5 55.6 %copy-start.11 = (f32[4,2048]{1,0:T(4,128)S(1)}, f32[4,2048]{1,0:T(4,128)}, u32[]{:S(2)}) copy-start(f32[4,2048]{1,0:T(4,128)} %param.14) | copy-start | bytes 98308
  6.5 466.7 %all-reduce.9.cloned.1.call-start = ((), (), s32[]{:S(2)}) async-start(), calls=%async_computation | async-start | bytes 131072 | tf_op jit(solution)/shard_map/psum | solution.py:149
  7.3 8.4 %collective-permute-start.1 = (f32[1,8,256]{2,1,0:T(8,128)S(1)}, f32[1,8,256]{2,1,0:T(8,128)S(1)}, u32[]{:S(2)}, u32[]{:S(2)}) collective-permute-start(f32[1,8,256]{2,1,0:T(8,128)S(1)} %get-tuple-element.35), channel_id=1, source_target_pairs={{0,16},{16,32},{32,48},{1,17},{17,33},{33,49},{2,18},{18,34},{34,5... | collective-permute-start | bytes 24584 | tf_op jit(solution)/shard_map/ppermute | solution.py:17
  10.8 5.8 %collective-permute-start = (f32[1,8,256]{2,1,0:T(8,128)S(1)}, f32[1,8,256]{2,1,0:T(8,128)S(1)}, u32[]{:S(2)}, u32[]{:S(2)}) collective-permute-start(f32[1,8,256]{2,1,0:T(8,128)S(1)} %get-tuple-element.34), channel_id=1, source_target_pairs={{16,0},{32,16},{48,32},{17,1},{33,17},{49,33},{18,2},{34,18},{50,3... | collective-permute-start | bytes 24584 | tf_op jit(solution)/shard_map/ppermute | solution.py:20
  16.6 11.5 %collective-permute-start.2 = (f32[10,1,256]{2,1,0:T(1,128)S(1)}, f32[10,1,256]{2,1,0:T(1,128)S(1)}, u32[]{:S(2)}, u32[]{:S(2)}) collective-permute-start(f32[10,1,256]{2,1,0:T(1,128)S(1)} %get-tuple-element.33), channel_id=1, source_target_pairs={{1,0},{2,1},{3,2},{4,3},{5,4},{6,5},{7,6},{8,7},{9,8},{10,9},{11,1... | collective-permute-start | bytes 30728 | tf_op jit(solution)/shard_map/ppermute | solution.py:20
  22.2 5.9 %collective-permute-start.3 = (f32[10,1,256]{2,1,0:T(1,128)S(1)}, f32[10,1,256]{2,1,0:T(1,128)S(1)}, u32[]{:S(2)}, u32[]{:S(2)}) collective-permute-start(f32[10,1,256]{2,1,0:T(1,128)S(1)} %get-tuple-element.32), channel_id=1, source_target_pairs={{0,1},{1,2},{2,3},{3,4},{4,5},{5,6},{6,7},{7,8},{8,9},{9,10},{10,1... | collective-permute-start | bytes 30728 | tf_op jit(solution)/shard_map/ppermute | solution.py:17
  29.5 6.5 %collective-permute-start.4 = (f32[4,1,8,256]{3,2,1,0:T(8,128)S(1)}, f32[4,1,8,256]{3,2,1,0:T(8,128)S(1)}, u32[]{:S(2)}, u32[]{:S(2)}) collective-permute-start(f32[4,1,8,256]{3,2,1,0:T(8,128)S(1)} %get-tuple-element.31), channel_id=1, source_target_pairs={{16,0},{32,16},{48,32},{17,1},{33,17},{49,33},{18,2},{34,18},{50,3... | collective-permute-start | bytes 98312 | tf_op jit(solution)/shard_map/ppermute | solution.py:20
  30.8 6.8 %collective-permute-start.5 = (f32[4,1,8,256]{3,2,1,0:T(8,128)S(1)}, f32[4,1,8,256]{3,2,1,0:T(8,128)S(1)}, u32[]{:S(2)}, u32[]{:S(2)}) collective-permute-start(f32[4,1,8,256]{3,2,1,0:T(8,128)S(1)} %get-tuple-element.30), channel_id=1, source_target_pairs={{0,16},{16,32},{32,48},{1,17},{17,33},{33,49},{2,18},{18,34},{34,5... | collective-permute-start | bytes 98312 | tf_op jit(solution)/shard_map/ppermute | solution.py:17
  37.6 6.7 %collective-permute-start.6 = (f32[4,10,1,256]{3,2,1,0:T(1,128)S(1)}, f32[4,10,1,256]{3,2,1,0:T(1,128)S(1)}, u32[]{:S(2)}, u32[]{:S(2)}) collective-permute-start(f32[4,10,1,256]{3,2,1,0:T(1,128)S(1)} %get-tuple-element.22), channel_id=1, source_target_pairs={{1,0},{2,1},{3,2},{4,3},{5,4},{6,5},{7,6},{8,7},{9,8},{10,9},{11,1... | collective-permute-start | bytes 122888 | tf_op jit(solution)/shard_map/ppermute | solution.py:20
  41.5 5.9 %collective-permute-start.7 = (f32[4,10,1,256]{3,2,1,0:T(1,128)S(1)}, f32[4,10,1,256]{3,2,1,0:T(1,128)S(1)}, u32[]{:S(2)}, u32[]{:S(2)}) collective-permute-start(f32[4,10,1,256]{3,2,1,0:T(1,128)S(1)} %get-tuple-element.23), channel_id=1, source_target_pairs={{0,1},{1,2},{2,3},{3,4},{4,5},{5,6},{6,7},{7,8},{8,9},{9,10},{10,1... | collective-permute-start | bytes 122888 | tf_op jit(solution)/shard_map/ppermute | solution.py:17
  47.7 6.2 %collective-permute-start.8 = (f32[4,1,8,256]{3,2,1,0:T(8,128)S(1)}, f32[4,1,8,256]{3,2,1,0:T(8,128)S(1)}, u32[]{:S(2)}, u32[]{:S(2)}) collective-permute-start(f32[4,1,8,256]{3,2,1,0:T(8,128)S(1)} %get-tuple-element.29), channel_id=1, source_target_pairs={{16,0},{32,16},{48,32},{17,1},{33,17},{49,33},{18,2},{34,18},{50,3... | collective-permute-start | bytes 98312 | tf_op jit(solution)/shard_map/ppermute | solution.py:20
  49.0 6.4 %collective-permute-start.9 = (f32[4,1,8,256]{3,2,1,0:T(8,128)S(1)}, f32[4,1,8,256]{3,2,1,0:T(8,128)S(1)}, u32[]{:S(2)}, u32[]{:S(2)}) collective-permute-start(f32[4,1,8,256]{3,2,1,0:T(8,128)S(1)} %get-tuple-element.28), channel_id=1, source_target_pairs={{0,16},{16,32},{32,48},{1,17},{17,33},{33,49},{2,18},{18,34},{34,5... | collective-permute-start | bytes 98312 | tf_op jit(solution)/shard_map/ppermute | solution.py:17
  55.5 7.0 %collective-permute-start.10 = (f32[4,10,1,256]{3,2,1,0:T(1,128)S(1)}, f32[4,10,1,256]{3,2,1,0:T(1,128)S(1)}, u32[]{:S(2)}, u32[]{:S(2)}) collective-permute-start(f32[4,10,1,256]{3,2,1,0:T(1,128)S(1)} %get-tuple-element.20), channel_id=1, source_target_pairs={{1,0},{2,1},{3,2},{4,3},{5,4},{6,5},{7,6},{8,7},{9,8},{10,9},{11,1... | collective-permute-start | bytes 122888 | tf_op jit(solution)/shard_map/ppermute | solution.py:20
  57.4 6.2 %collective-permute-start.11 = (f32[4,10,1,256]{3,2,1,0:T(1,128)S(1)}, f32[4,10,1,256]{3,2,1,0:T(1,128)S(1)}, u32[]{:S(2)}, u32[]{:S(2)}) collective-permute-start(f32[4,10,1,256]{3,2,1,0:T(1,128)S(1)} %get-tuple-element.21), channel_id=1, source_target_pairs={{0,1},{1,2},{2,3},{3,4},{4,5},{5,6},{6,7},{7,8},{8,9},{9,10},{10,1... | collective-permute-start | bytes 122888 | tf_op jit(solution)/shard_map/ppermute | solution.py:17
  222.6 114.2 %copy-start.2 = (f32[8,8,256]{2,1,0:T(8,128)S(1)}, f32[8,8,256]{2,1,0:T(8,128)}, u32[]{:S(2)}) copy-start(f32[8,8,256]{2,1,0:T(8,128)} %copy-done.1) | copy-start | bytes 196612
  222.6 114.2 %copy-start.4 = (f32[8,8,256]{2,1,0:T(8,128)S(1)}, f32[8,8,256]{2,1,0:T(8,128)}, u32[]{:S(2)}) copy-start(f32[8,8,256]{2,1,0:T(8,128)} %copy-done.3) | copy-start | bytes 196612
  222.6 114.2 %copy-start.6 = (f32[8,8,256]{2,1,0:T(8,128)S(1)}, f32[8,8,256]{2,1,0:T(8,128)}, u32[]{:S(2)}) copy-start(f32[8,8,256]{2,1,0:T(8,128)} %copy-done.5) | copy-start | bytes 196612
  222.6 114.2 %copy-start.8 = (f32[8,8,256]{2,1,0:T(8,128)S(1)}, f32[8,8,256]{2,1,0:T(8,128)}, u32[]{:S(2)}) copy-start(f32[8,8,256]{2,1,0:T(8,128)} %copy-done.7) | copy-start | bytes 196612
  222.7 114.2 %copy-start.10 = (f32[8,8,256]{2,1,0:T(8,128)S(1)}, f32[8,8,256]{2,1,0:T(8,128)}, u32[]{:S(2)}) copy-start(f32[8,8,256]{2,1,0:T(8,128)} %copy-done.9) | copy-start | bytes 196612
  319.5 5.9 %collective-permute-start.12 = (f32[4,1,8,256]{3,2,1,0:T(8,128)S(1)}, f32[4,1,8,256]{3,2,1,0:T(8,128)S(1)}, u32[]{:S(2)}, u32[]{:S(2)}) collective-permute-start(f32[4,1,8,256]{3,2,1,0:T(8,128)S(1)} %get-tuple-element.27), channel_id=1, source_target_pairs={{16,0},{32,16},{48,32},{17,1},{33,17},{49,33},{18,2},{34,18},{50,3... | collective-permute-start | bytes 98312 | tf_op jit(solution)/shard_map/ppermute | solution.py:20
  320.8 6.1 %collective-permute-start.13 = (f32[4,1,8,256]{3,2,1,0:T(8,128)S(1)}, f32[4,1,8,256]{3,2,1,0:T(8,128)S(1)}, u32[]{:S(2)}, u32[]{:S(2)}) collective-permute-start(f32[4,1,8,256]{3,2,1,0:T(8,128)S(1)} %get-tuple-element.26), channel_id=1, source_target_pairs={{0,16},{16,32},{32,48},{1,17},{17,33},{33,49},{2,18},{18,34},{34,5... | collective-permute-start | bytes 98312 | tf_op jit(solution)/shard_map/ppermute | solution.py:17
  327.0 5.9 %collective-permute-start.14 = (f32[4,10,1,256]{3,2,1,0:T(1,128)S(1)}, f32[4,10,1,256]{3,2,1,0:T(1,128)S(1)}, u32[]{:S(2)}, u32[]{:S(2)}) collective-permute-start(f32[4,10,1,256]{3,2,1,0:T(1,128)S(1)} %get-tuple-element.18), channel_id=1, source_target_pairs={{1,0},{2,1},{3,2},{4,3},{5,4},{6,5},{7,6},{8,7},{9,8},{10,9},{11,1... | collective-permute-start | bytes 122888 | tf_op jit(solution)/shard_map/ppermute | solution.py:20
  330.9 5.9 %collective-permute-start.15 = (f32[4,10,1,256]{3,2,1,0:T(1,128)S(1)}, f32[4,10,1,256]{3,2,1,0:T(1,128)S(1)}, u32[]{:S(2)}, u32[]{:S(2)}) collective-permute-start(f32[4,10,1,256]{3,2,1,0:T(1,128)S(1)} %get-tuple-element.19), channel_id=1, source_target_pairs={{0,1},{1,2},{2,3},{3,4},{4,5},{5,6},{6,7},{7,8},{8,9},{9,10},{10,1... | collective-permute-start | bytes 122888 | tf_op jit(solution)/shard_map/ppermute | solution.py:17
  337.1 6.2 %collective-permute-start.16 = (f32[4,1,8,256]{3,2,1,0:T(8,128)S(1)}, f32[4,1,8,256]{3,2,1,0:T(8,128)S(1)}, u32[]{:S(2)}, u32[]{:S(2)}) collective-permute-start(f32[4,1,8,256]{3,2,1,0:T(8,128)S(1)} %get-tuple-element.25), channel_id=1, source_target_pairs={{16,0},{32,16},{48,32},{17,1},{33,17},{49,33},{18,2},{34,18},{50,3... | collective-permute-start | bytes 98312 | tf_op jit(solution)/shard_map/ppermute | solution.py:20
  338.4 6.4 %collective-permute-start.17 = (f32[4,1,8,256]{3,2,1,0:T(8,128)S(1)}, f32[4,1,8,256]{3,2,1,0:T(8,128)S(1)}, u32[]{:S(2)}, u32[]{:S(2)}) collective-permute-start(f32[4,1,8,256]{3,2,1,0:T(8,128)S(1)} %get-tuple-element.24), channel_id=1, source_target_pairs={{0,16},{16,32},{32,48},{1,17},{17,33},{33,49},{2,18},{18,34},{34,5... | collective-permute-start | bytes 98312 | tf_op jit(solution)/shard_map/ppermute | solution.py:17
  344.9 5.9 %collective-permute-start.18 = (f32[4,10,1,256]{3,2,1,0:T(1,128)S(1)}, f32[4,10,1,256]{3,2,1,0:T(1,128)S(1)}, u32[]{:S(2)}, u32[]{:S(2)}) collective-permute-start(f32[4,10,1,256]{3,2,1,0:T(1,128)S(1)} %get-tuple-element.16), channel_id=1, source_target_pairs={{1,0},{2,1},{3,2},{4,3},{5,4},{6,5},{7,6},{8,7},{9,8},{10,9},{11,1... | collective-permute-start | bytes 122888 | tf_op jit(solution)/shard_map/ppermute | solution.py:20
  346.9 5.9 %collective-permute-start.19 = (f32[4,10,1,256]{3,2,1,0:T(1,128)S(1)}, f32[4,10,1,256]{3,2,1,0:T(1,128)S(1)}, u32[]{:S(2)}, u32[]{:S(2)}) collective-permute-start(f32[4,10,1,256]{3,2,1,0:T(1,128)S(1)} %get-tuple-element.17), channel_id=1, source_target_pairs={{0,1},{1,2},{2,3},{3,4},{4,5},{5,6},{6,7},{7,8},{8,9},{9,10},{10,1... | collective-permute-start | bytes 122888 | tf_op jit(solution)/shard_map/ppermute | solution.py:17
  353.0 6.5 %collective-permute-start.20 = (f32[8,1,8,256]{3,2,1,0:T(8,128)S(1)}, f32[8,1,8,256]{3,2,1,0:T(8,128)S(1)}, u32[]{:S(2)}, u32[]{:S(2)}) collective-permute-start(f32[8,1,8,256]{3,2,1,0:T(8,128)S(1)} %get-tuple-element.15), channel_id=1, source_target_pairs={{16,0},{32,16},{48,32},{17,1},{33,17},{49,33},{18,2},{34,18},{50,3... | collective-permute-start | bytes 196616 | tf_op jit(solution)/shard_map/ppermute | solution.py:20
  354.3 6.7 %collective-permute-start.21 = (f32[8,1,8,256]{3,2,1,0:T(8,128)S(1)}, f32[8,1,8,256]{3,2,1,0:T(8,128)S(1)}, u32[]{:S(2)}, u32[]{:S(2)}) collective-permute-start(f32[8,1,8,256]{3,2,1,0:T(8,128)S(1)} %get-tuple-element.14), channel_id=1, source_target_pairs={{0,16},{16,32},{32,48},{1,17},{17,33},{33,49},{2,18},{18,34},{34,5... | collective-permute-start | bytes 196616 | tf_op jit(solution)/shard_map/ppermute | solution.py:17
  361.2 6.3 %collective-permute-start.22 = (f32[8,10,1,256]{3,2,1,0:T(1,128)S(1)}, f32[8,10,1,256]{3,2,1,0:T(1,128)S(1)}, u32[]{:S(2)}, u32[]{:S(2)}) collective-permute-start(f32[8,10,1,256]{3,2,1,0:T(1,128)S(1)} %get-tuple-element.12), channel_id=1, source_target_pairs={{1,0},{2,1},{3,2},{4,3},{5,4},{6,5},{7,6},{8,7},{9,8},{10,9},{11,1... | collective-permute-start | bytes 245768 | tf_op jit(solution)/shard_map/ppermute | solution.py:20
  363.1 6.3 %collective-permute-start.23 = (f32[8,10,1,256]{3,2,1,0:T(1,128)S(1)}, f32[8,10,1,256]{3,2,1,0:T(1,128)S(1)}, u32[]{:S(2)}, u32[]{:S(2)}) collective-permute-start(f32[8,10,1,256]{3,2,1,0:T(1,128)S(1)} %get-tuple-element.13), channel_id=1, source_target_pairs={{0,1},{1,2},{2,3},{3,4},{4,5},{5,6},{6,7},{7,8},{8,9},{9,10},{10,1... | collective-permute-start | bytes 245768 | tf_op jit(solution)/shard_map/ppermute | solution.py:17
  (5 other events, 163.4 us)
Sparse Core Ops, SparseCore 0:
  370.7 102.5 all-reduce.8
